TPU v7x, 256 devices: a whole 4x4x8 slice. The times are simulated.
256 devices in a mesh: cell: 32 (over y, z), lt: 8 (over x, core).
Axes of the slice: x: 4, y: 4, z: 8, core: 2. Of those that a mesh axis runs over, the one named last changes fastest.
Arguments:
- field: float32 [8, 80, 1048576], P('lt', None, 'cell'), may hold values from -54 to 54
- level_start: float32 [80, 24], replicated, may hold values from -6 to 6
- time_start: float32 [8, 6], replicated, may hold values from -6 to 6
Outputs:
- core: float32 [6, 24, 1048576], P(None, 'lt', 'cell')
- level_basis: float32 [80, 24], replicated
- time_basis: float32 [8, 6], replicated
All inputs are finite; a program needn't handle non-finite values.
Results may differ from a plain program's by a relative error of at most 0.0003.
Values sent between devices are 32-bit elements; how exact they have to be, the bound alone decides.
No kernel may reach another device: no remote copies, remote signals or barrier semaphores. Data moves between devices by JAX's collectives and lax.ppermute only.
A program may use at most 64 MiB of HBM per device.

v0:
```python
import jax
import jax.numpy as jnp
from jax import lax
from jax.sharding import PartitionSpec as P

ITERS = 3
highest = lax.Precision.HIGHEST


def orthonormal(matrix):
    square = jnp.dot(matrix.T, matrix, precision=highest)
    factor = jnp.linalg.cholesky(square)
    return lax.linalg.triangular_solve(
        factor, matrix, left_side=False, lower=True, transpose_a=True
    )


def body(field, level_start, time_start):
    level_basis = orthonormal(level_start)
    for step in range(ITERS):
        projected = jnp.einsum("slc,lr->src", field, level_basis, precision=highest)
        local_term = jnp.einsum("slc,src->lr", field, projected, precision=highest)
        applied = lax.psum(local_term, ("cell", "lt"))
        level_basis = orthonormal(applied)
    reduced = jnp.einsum("lr,slc->src", level_basis, field, precision=highest)
    regrouped = lax.all_to_all(reduced, "lt", split_axis=1, concat_axis=0, tiled=True)
    time_local = jnp.einsum("src,trc->st", regrouped, regrouped, precision=highest)
    time_gram = lax.psum(time_local, ("cell", "lt"))
    time_basis = orthonormal(time_start)
    for step in range(ITERS):
        time_basis = orthonormal(jnp.dot(time_gram, time_basis, precision=highest))
    core_local = jnp.einsum("sq,src->qrc", time_basis, regrouped, precision=highest)
    return (core_local, level_basis, time_basis)


def solution(mesh):
    placed = (P("lt", None, "cell"), P(), P())
    return jax.shard_map(
        body,
        mesh=mesh,
        in_specs=placed,
        out_specs=(P(None, "lt", "cell"), P(), P()),
        check_vma=False,
    )
```

profile of v0, /device:TPU:1, one launch (start us, length us, event | category | flops | bytes accessed | tf_op | source)
XLA Modules:
  0.0 481.1 jit_solution(1306957833141414839)
XLA Ops:
  0.6 0.7 copy-done
  1.6 2.2 cholesky.146
  3.8 0.6 compare_reduce_fusion.7
  4.4 0.6 fusion.29
  5.1 1.8 custom-call.16
  6.9 0.2 convolution_bitcast_fusion.4
  7.2 7.9 %fusion.11 = f32[24,32768]{1,0:T(8,128)S(1)} fusion(f32[80,24]{0,1:T(8,128)S(1)} %convolution_bitcast_fusion.4, f32[1,80,32768]{2,1,0:T(8,128)} %param.9), kind=kOutput, calls=%fused_computation.12 | convolution fusion | flops 754974720 | bytes 13639168 | tf_op jit(solution)/shard_map/slc,lr->src/dot_general | solution.py:21
  15.1 8.3 %fusion.17 = f32[80,24]{0,1:T(8,128)S(1)} fusion(f32[24,32768]{1,0:T(8,128)S(1)} %fusion.11, f32[1,80,32768]{2,1,0:T(8,128)S(1)} %copy-done.1), kind=kOutput, calls=%fused_computation.18 | convolution fusion | flops 754974720 | bytes 13639168 | tf_op jit(solution)/shard_map/slc,src->lr/dot_general | solution.py:22
  23.3 81.7 %psum.28 = f32[80,24]{0,1:T(8,128)S(1)} all-reduce(f32[80,24]{0,1:T(8,128)S(1)} %fusion.17), channel_id=1, replica_groups=mesh['cell'=32,'lt'=8] {'cell','lt'}, use_global_device_ids=true, to_apply=%region_2.5 | all-reduce | flops 1920 | bytes 15360 | tf_op jit(solution)/shard_map/psum | solution.py:23
  105.2 2.2 cholesky.157
  107.5 0.6 compare_reduce_fusion.6
  108.1 0.6 fusion.30
  108.8 1.8 custom-call.17
  110.6 0.2 convolution_bitcast_fusion.3
  110.8 7.7 %fusion.7 = f32[24,32768]{1,0:T(8,128)S(1)} fusion(f32[80,24]{0,1:T(8,128)S(1)} %convolution_bitcast_fusion.3, f32[1,80,32768]{2,1,0:T(8,128)} %param.9), kind=kOutput, calls=%fused_computation.8 | convolution fusion | flops 754974720 | bytes 13639168 | tf_op jit(solution)/shard_map/slc,lr->src/dot_general | solution.py:21
  118.6 10.9 %fusion.20 = f32[80,24]{0,1:T(8,128)S(1)} fusion(f32[24,32768]{1,0:T(8,128)S(1)} %fusion.7, f32[1,80,32768]{2,1,0:T(8,128)} %param.9), kind=kOutput, calls=%fused_computation.19 | convolution fusion | flops 754974720 | bytes 13639168 | tf_op jit(solution)/shard_map/slc,src->lr/dot_general | solution.py:22
  129.5 73.0 %psum.29 = f32[80,24]{0,1:T(8,128)S(1)} all-reduce(f32[80,24]{0,1:T(8,128)S(1)} %fusion.20), channel_id=1, replica_groups=mesh['cell'=32,'lt'=8] {'cell','lt'}, use_global_device_ids=true, to_apply=%region_3.6 | all-reduce | flops 1920 | bytes 15360 | tf_op jit(solution)/shard_map/psum | solution.py:23
  202.7 2.2 cholesky.168
  204.9 0.6 compare_reduce_fusion.5
  205.6 0.6 fusion.31
  206.2 1.8 custom-call.18
  208.1 0.2 convolution_bitcast_fusion.2
  208.3 7.7 %fusion.3 = f32[24,32768]{1,0:T(8,128)S(1)} fusion(f32[80,24]{0,1:T(8,128)S(1)} %convolution_bitcast_fusion.2, f32[1,80,32768]{2,1,0:T(8,128)} %param.9), kind=kOutput, calls=%fused_computation.4 | convolution fusion | flops 754974720 | bytes 13639168 | tf_op jit(solution)/shard_map/slc,lr->src/dot_general | solution.py:21
  216.0 10.9 %fusion.23 = f32[80,24]{0,1:T(8,128)S(1)} fusion(f32[24,32768]{1,0:T(8,128)S(1)} %fusion.3, f32[1,80,32768]{2,1,0:T(8,128)} %param.9), kind=kOutput, calls=%fused_computation.20 | convolution fusion | flops 754974720 | bytes 13639168 | tf_op jit(solution)/shard_map/slc,src->lr/dot_general | solution.py:22
  226.9 74.1 %psum.30 = f32[80,24]{0,1:T(8,128)S(1)} all-reduce(f32[80,24]{0,1:T(8,128)S(1)} %fusion.23), channel_id=1, replica_groups=mesh['cell'=32,'lt'=8] {'cell','lt'}, use_global_device_ids=true, to_apply=%region_4.7 | all-reduce | flops 1920 | bytes 15360 | tf_op jit(solution)/shard_map/psum | solution.py:23
  301.2 2.2 cholesky.179
  303.4 0.6 compare_reduce_fusion.4
  304.1 0.6 fusion.32
  304.7 1.8 custom-call.19
  306.6 0.2 convolution_bitcast_fusion.1
  306.8 7.8 %convolution_bitcast_fusion = f32[1,24,32768]{2,1,0:T(8,128)S(1)} fusion(f32[80,24]{0,1:T(8,128)S(1)} %convolution_bitcast_fusion.1, f32[1,80,32768]{2,1,0:T(8,128)} %param.9), kind=kOutput, calls=%fused_computation | convolution fusion | flops 754974720 | bytes 13639168 | tf_op jit(solution)/shard_map/lr,slc->src/dot_general | solution.py:25
  314.6 4.9 %copy.44 = f32[1,24,32768]{2,0,1:T(1,128)} copy(f32[1,24,32768]{2,1,0:T(8,128)S(1)} %convolution_bitcast_fusion) | data formatting | bytes 6291456 | tf_op jit(solution)/shard_map/lr,slc->src/transpose | solution.py:25
  319.5 5.6 %all-to-all-start = ((f32[1,24,32768]{2,0,1:T(1,128)}), f32[1,24,32768]{2,0,1:T(1,128)}, u32[]{:S(2)}, u32[]{:S(2)}) async-start(f32[1,24,32768]{2,0,1:T(1,128)} %copy.44), calls=%async_computation | async-start | bytes 6291456 | tf_op jit(solution)/shard_map/all_to_all | solution.py:26
  325.4 0.5 cholesky.190
  325.9 0.6 compare_reduce_fusion.3
  326.6 0.6 fusion.47
  327.2 0.5 custom-call.20
  327.7 0.2 convolution_bitcast_fusion.7
  327.9 34.3 %all-to-all-done = f32[1,24,32768]{2,0,1:T(1,128)} async-done(((f32[1,24,32768]{2,0,1:T(1,128)}), f32[1,24,32768]{2,0,1:T(1,128)}, u32[]{:S(2)}, u32[]{:S(2)}) %all-to-all-start) | async-done | bytes 3145760 | tf_op jit(solution)/shard_map/all_to_all | solution.py:26
  362.2 9.9 %reduce.8 = f32[24,32768]{1,0:T(8,128)S(1)} reduce(f32[1,24,32768]{2,0,1:T(1,128)} %all-to-all-done, f32[]{:T(128)} %constant.59), dimensions={0}, to_apply=%all_to_all.4.reduce_sub_computation | reduce | bytes 6291460 | tf_op jit(solution)/shard_map/all_to_all | solution.py:26
  372.1 3.3 all_to_all.10
  375.4 12.4 %fusion.26 = f32[8,8]{1,0:T(8,128)S(1)} fusion(f32[8,3,32768]{2,1,0:T(4,128)} %all_to_all.10), kind=kOutput, calls=%fused_computation.25 | convolution fusion | flops 75497472 | bytes 3145984 | tf_op jit(solution)/shard_map/src,trc->st/dot_general | solution.py:27
  387.9 73.7 %psum.31 = f32[8,8]{1,0:T(8,128)S(1)} all-reduce(f32[8,8]{1,0:T(8,128)S(1)} %fusion.26), channel_id=1, replica_groups=mesh['cell'=32,'lt'=8] {'cell','lt'}, use_global_device_ids=true, to_apply=%region_5.8 | all-reduce | flops 64 | bytes 512 | tf_op jit(solution)/shard_map/psum | solution.py:28
  461.7 0.2 fusion.73
  462.0 0.5 cholesky.201
  462.6 0.6 compare_reduce_fusion.2
  463.2 0.6 fusion.48
  463.9 0.5 custom-call.21
  464.3 0.2 convolution_bitcast_fusion.6
  464.7 0.2 fusion.75
  465.0 0.5 cholesky.212
  465.6 0.6 compare_reduce_fusion.1
  466.2 0.6 fusion.49
  466.9 0.5 custom-call.22
  467.3 0.2 convolution_bitcast_fusion.5
  467.7 0.2 fusion.77
  468.0 0.5 cholesky.223
  468.6 0.6 compare_reduce_fusion
  469.2 0.6 fusion.50
  469.9 0.5 custom-call.23
  470.3 0.2 fusion.51
  470.5 6.4 %fusion.13 = f32[6,3,32768]{2,0,1:T(8,128)S(1)} fusion(f32[8,3,32768]{2,1,0:T(4,128)} %all_to_all.10, f32[6,8]{1,0:T(8,128)S(1)} %fusion.51), kind=kOutput, calls=%fused_computation.14 | convolution fusion | flops 56623104 | bytes 5505216 | tf_op jit(solution)/shard_map/sq,src->qrc/dot_general | solution.py:32
  477.0 3.3 copy.56
  480.3 0.7 copy.57
  (39 shorter events, 2.2 us)
Async XLA Ops:
  0.6 0.7 copy-start
  7.2 7.9 %copy-start.1 = (f32[1,80,32768]{2,1,0:T(8,128)S(1)}, f32[1,80,32768]{2,1,0:T(8,128)}, u32[]{:S(2)}) copy-start(f32[1,80,32768]{2,1,0:T(8,128)} %param.9) | copy-start | bytes 31457284
  306.8 7.8 %copy-start.2 = (f32[80,24]{0,1:T(8,128)}, f32[80,24]{0,1:T(8,128)S(1)}, u32[]{:S(2)}) copy-start(f32[80,24]{0,1:T(8,128)S(1)} %convolution_bitcast_fusion.1) | copy-start | bytes 23044
  319.5 5.6 %copy-start.3 = (f32[8,6]{1,0:T(8,128)S(1)}, f32[8,6]{1,0:T(8,128)}, u32[]{:S(2)}) copy-start(f32[8,6]{1,0:T(8,128)} %param.11) | copy-start | bytes 580
  319.5 42.7 %all-to-all-start = ((f32[1,24,32768]{2,0,1:T(1,128)}), f32[1,24,32768]{2,0,1:T(1,128)}, u32[]{:S(2)}, u32[]{:S(2)}) async-start(f32[1,24,32768]{2,0,1:T(1,128)} %copy.44), calls=%async_computation | async-start | bytes 6291456 | tf_op jit(solution)/shard_map/all_to_all | solution.py:26
where the time goes:
time: 490 us; the launch traced here: 481 us
  blocking collectives  302 us (62%)
  matrix products  83.4 us (17%)
  other arithmetic  40.8 us (8%)
  waiting for transfers between devices  34.3 us (7%)
  local copies, waits for them, and re-layouts  13.6 us (3%)
  starting transfers between devices  5.56 us (1%)
    psum x3, blocking collectives, body(): applied = lax.psum(local_term, ('cell', 'lt'))  229 us
    psum x1, blocking collectives, body(): time_gram = lax.psum(time_local, ('cell', 'lt'))  73.7 us
    all_to_all x1, waiting for transfers between devices, body(): lax.all_to_all(reduced, 'lt', split_axis=1, concat_axis=0, tiled=True)  34.3 us
    dot_general x3, matrix products, body(): local_term = jnp.einsum('slc,src->lr', field, projected, precision=highest)  30 us
    dot_general x3, matrix products, body(): projected = jnp.einsum('slc,lr->src', field, level_basis, precision=highest)  23.4 us
    another operation x24, other arithmetic, orthonormal(): factor = jnp.linalg.cholesky(square)  16.4 us
    another operation x16, other arithmetic, orthonormal(): lax.linalg.triangular_solve(factor, matrix, left_side=False, lower=True,...  14.4 us
    dot_general x1, matrix products, body(): jnp.einsum('src,trc->st', regrouped, regrouped, precision=highest)  12.4 us
  transfers between devices with their start and end apart: 1, of which 1 were waited for; matrix products, arithmetic and copies ran while one was open for 1% of the time, Pallas kernels for 0%

commit v1 on v0

--- a/solution.py
+++ b/solution.py
@@ -1,3 +1,4 @@
+import functools
 import jax
 import jax.numpy as jnp
 from jax import lax
@@ -5,6 +6,14 @@
 
 ITERS = 3
 highest = lax.Precision.HIGHEST
+
+
+def axis_part_spread(x0, named_axis):
+    block_now = lax.all_gather(x0, named_axis)
+    return jnp.sum(block_now, 0)
+
+
+convert_the_rates = functools.partial(axis_part_spread, named_axis=("cell", "lt"))
 
 
 def orthonormal(matrix):
@@ -20,7 +29,7 @@
     for step in range(ITERS):
         projected = jnp.einsum("slc,lr->src", field, level_basis, precision=highest)
         local_term = jnp.einsum("slc,src->lr", field, projected, precision=highest)
-        applied = lax.psum(local_term, ("cell", "lt"))
+        applied = convert_the_rates(local_term)
         level_basis = orthonormal(applied)
     reduced = jnp.einsum("lr,slc->src", level_basis, field, precision=highest)
     regrouped = lax.all_to_all(reduced, "lt", split_axis=1, concat_axis=0, tiled=True)

time: 490 us -> 602 us (1.23)
  waiting for transfers between devices: 34.3 us -> 352 us
  blocking collectives: 302 us -> 75.5 us
  between operations: 1.09 us -> 14.2 us
  other arithmetic: 40.8 us -> 47.4 us
    all_gather x0 -> x3, waiting for transfers between devices: none -> 318 us  [axis_part_spread(): block_now = lax.all_gather(x0, named_axis)]
    psum x3 -> x0, blocking collectives: 229 us -> none  [body(): applied = lax.psum(local_term, ('cell', 'lt'))]
    reduce_sum x0 -> x3, other arithmetic: none -> 6.57 us  [axis_part_spread(): return jnp.sum(block_now, 0)]
  transfers between devices with their start and end apart: 1 -> 4, of which waited for: 1 -> 4; matrix products, arithmetic and copies ran while one was open for 1% -> 0% of each run, Pallas kernels for 0% -> 0%
where the time goes in v1:
time: 602 us; the launch traced here: 594 us
  waiting for transfers between devices  352 us (58%)
  matrix products  85.3 us (14%)
  blocking collectives  75.5 us (13%)
  other arithmetic  47.4 us (8%)
  between operations  14.2 us (2%)
  local copies, waits for them, and re-layouts  13.5 us (2%)
    all_gather x3, waiting for transfers between devices, axis_part_spread(): block_now = lax.all_gather(x0, named_axis)  318 us
    psum x1, blocking collectives, body(): time_gram = lax.psum(time_local, ('cell', 'lt'))  75.5 us
    all_to_all x1, waiting for transfers between devices, body(): lax.all_to_all(reduced, 'lt', split_axis=1, concat_axis=0, tiled=True)  34.3 us
    dot_general x3, matrix products, body(): local_term = jnp.einsum('slc,src->lr', field, projected, precision=highest)  31.9 us
    dot_general x3, matrix products, body(): projected = jnp.einsum('slc,lr->src', field, level_basis, precision=highest)  23.4 us
    another operation x24, other arithmetic, orthonormal(): factor = jnp.linalg.cholesky(square)  16.4 us
    another operation x16, other arithmetic, orthonormal(): lax.linalg.triangular_solve(factor, matrix, left_side=False, lower=True,...  14.4 us
    dot_general x1, matrix products, body(): jnp.einsum('src,trc->st', regrouped, regrouped, precision=highest)  12.4 us
  transfers between devices with their start and end apart: 4, of which 4 were waited for; matrix products, arithmetic and copies ran while one was open for 0% of the time, Pallas kernels for 0%

profile of v1, /device:TPU:1, one launch (start us, length us, event | category | flops | bytes accessed | tf_op | source)
XLA Modules:
  0.0 593.6 jit_solution(6938460275924661301)
XLA Ops:
  7.2 0.7 copy-done
  8.1 2.2 cholesky.146
  10.3 0.6 compare_reduce_fusion.7
  11.0 0.6 fusion.29
  11.6 1.8 custom-call.16
  13.5 0.2 convolution_bitcast_fusion.4
  13.7 7.9 %fusion.11 = f32[24,32768]{1,0:T(8,128)S(1)} fusion(f32[80,24]{0,1:T(8,128)S(1)} %convolution_bitcast_fusion.4, f32[1,80,32768]{2,1,0:T(8,128)} %param.9), kind=kOutput, calls=%fused_computation.12 | convolution fusion | flops 754974720 | bytes 13639168 | tf_op jit(solution)/shard_map/slc,lr->src/dot_general | solution.py:30
  21.6 8.9 %fusion.17 = f32[1,80,24]{1,2,0:T(8,128)} fusion(f32[24,32768]{1,0:T(8,128)S(1)} %fusion.11, f32[1,80,32768]{2,1,0:T(8,128)S(1)} %copy-done.1), kind=kOutput, calls=%fused_computation.18 | convolution fusion | flops 754974720 | bytes 13639168 | tf_op jit(solution)/shard_map/slc,src->lr/dot_general | solution.py:31
  30.5 0.2 all-gather.12.cloned.1.call-start
  30.7 109.3 %all-gather.10.cloned.1.call-done = f32[256,80,24]{1,2,0:T(8,128)} async-done(((f32[1,80,24]{1,2,0:T(8,128)}), f32[256,80,24]{1,2,0:T(8,128)}) %all-gather.10.cloned.1.call-update) | async-done | bytes 1966096 | tf_op jit(solution)/shard_map/all_gather | solution.py:12
  140.0 2.2 reduce_sum.27
  142.4 2.2 cholesky.157
  144.7 0.6 compare_reduce_fusion.6
  145.3 0.6 fusion.30
  146.0 1.8 custom-call.17
  147.8 0.2 convolution_bitcast_fusion.3
  148.0 7.7 %fusion.7 = f32[24,32768]{1,0:T(8,128)S(1)} fusion(f32[80,24]{0,1:T(8,128)S(1)} %convolution_bitcast_fusion.3, f32[1,80,32768]{2,1,0:T(8,128)} %param.9), kind=kOutput, calls=%fused_computation.8 | convolution fusion | flops 754974720 | bytes 13639168 | tf_op jit(solution)/shard_map/slc,lr->src/dot_general | solution.py:30
  155.8 11.5 %fusion.20 = f32[1,80,24]{1,2,0:T(8,128)} fusion(f32[24,32768]{1,0:T(8,128)S(1)} %fusion.7, f32[1,80,32768]{2,1,0:T(8,128)} %param.9), kind=kOutput, calls=%fused_computation.19 | convolution fusion | flops 754974720 | bytes 13639168 | tf_op jit(solution)/shard_map/slc,src->lr/dot_general | solution.py:31
  167.3 0.3 all-gather.14.cloned.1.call-start
  167.6 104.1 %all-gather.12.cloned.1.call-done = f32[256,80,24]{1,2,0:T(8,128)} async-done(((f32[1,80,24]{1,2,0:T(8,128)}), f32[256,80,24]{1,2,0:T(8,128)}) %all-gather.12.cloned.1.call-update) | async-done | bytes 1966096 | tf_op jit(solution)/shard_map/all_gather | solution.py:12
  271.7 2.2 reduce_sum.28
  274.1 2.2 cholesky.168
  276.3 0.6 compare_reduce_fusion.5
  276.9 0.6 fusion.31
  277.6 1.8 custom-call.18
  279.4 0.2 convolution_bitcast_fusion.2
  279.7 7.7 %fusion.3 = f32[24,32768]{1,0:T(8,128)S(1)} fusion(f32[80,24]{0,1:T(8,128)S(1)} %convolution_bitcast_fusion.2, f32[1,80,32768]{2,1,0:T(8,128)} %param.9), kind=kOutput, calls=%fused_computation.4 | convolution fusion | flops 754974720 | bytes 13639168 | tf_op jit(solution)/shard_map/slc,lr->src/dot_general | solution.py:30
  287.4 11.5 %fusion.23 = f32[1,80,24]{1,2,0:T(8,128)} fusion(f32[24,32768]{1,0:T(8,128)S(1)} %fusion.3, f32[1,80,32768]{2,1,0:T(8,128)} %param.9), kind=kOutput, calls=%fused_computation.20 | convolution fusion | flops 754974720 | bytes 13639168 | tf_op jit(solution)/shard_map/slc,src->lr/dot_general | solution.py:31
  298.9 104.3 %all-gather.14.cloned.1.call-done = f32[256,80,24]{1,2,0:T(8,128)} async-done(((f32[1,80,24]{1,2,0:T(8,128)}), f32[256,80,24]{1,2,0:T(8,128)}) %all-gather.14.cloned.1.call-update) | async-done | bytes 1966096 | tf_op jit(solution)/shard_map/all_gather | solution.py:12
  403.3 2.2 reduce_sum.29
  405.7 2.2 cholesky.179
  407.9 0.6 compare_reduce_fusion.4
  408.6 0.6 fusion.32
  409.2 1.8 custom-call.19
  411.1 0.2 convolution_bitcast_fusion.1
  411.3 7.8 %convolution_bitcast_fusion = f32[1,24,32768]{2,1,0:T(8,128)S(1)} fusion(f32[80,24]{0,1:T(8,128)S(1)} %convolution_bitcast_fusion.1, f32[1,80,32768]{2,1,0:T(8,128)} %param.9), kind=kOutput, calls=%fused_computation | convolution fusion | flops 754974720 | bytes 13639168 | tf_op jit(solution)/shard_map/lr,slc->src/dot_general | solution.py:34
  419.1 4.9 copy.44
  424.0 5.1 all-to-all-start
  429.5 0.5 cholesky.190
  430.0 0.6 compare_reduce_fusion.3
  430.7 0.6 fusion.47
  431.3 0.5 custom-call.20
  432.0 34.3 %all-to-all-done = f32[1,24,32768]{2,0,1:T(1,128)} async-done(((f32[1,24,32768]{2,0,1:T(1,128)}), f32[1,24,32768]{2,0,1:T(1,128)}, u32[]{:S(2)}, u32[]{:S(2)}) %all-to-all-start) | async-done | bytes 3145760 | tf_op jit(solution)/shard_map/all_to_all | solution.py:35
  466.3 9.9 %reduce.11 = f32[24,32768]{1,0:T(8,128)S(1)} reduce(f32[1,24,32768]{2,0,1:T(1,128)} %all-to-all-done, f32[]{:T(128)} %constant.61), dimensions={0}, to_apply=%all_to_all.4.reduce_sub_computation | reduce | bytes 6291460 | tf_op jit(solution)/shard_map/all_to_all | solution.py:35
  476.2 3.3 all_to_all.10
  479.5 12.4 %fusion.26 = f32[8,8]{1,0:T(8,128)S(1)} fusion(f32[8,3,32768]{2,1,0:T(4,128)} %all_to_all.10), kind=kOutput, calls=%fused_computation.25 | convolution fusion | flops 75497472 | bytes 3145984 | tf_op jit(solution)/shard_map/src,trc->st/dot_general | solution.py:36
  491.9 75.5 %psum.7 = f32[8,8]{1,0:T(8,128)S(1)} all-reduce(f32[8,8]{1,0:T(8,128)S(1)} %fusion.26), channel_id=1, replica_groups=mesh['cell'=32,'lt'=8] {'cell','lt'}, use_global_device_ids=true, to_apply=%region_5.8 | all-reduce | flops 64 | bytes 512 | tf_op jit(solution)/shard_map/psum | solution.py:37
  567.9 0.5 cholesky.201
  568.5 0.6 compare_reduce_fusion.2
  569.1 0.6 fusion.48
  569.8 0.5 custom-call.21
  570.6 0.2 fusion.75
  570.9 0.5 cholesky.212
  571.5 0.6 compare_reduce_fusion.1
  572.1 0.6 fusion.49
  572.8 0.5 custom-call.22
  573.6 0.2 fusion.77
  573.9 0.5 cholesky.223
  574.5 0.6 compare_reduce_fusion
  575.2 0.6 fusion.50
  575.8 0.5 custom-call.23
  576.5 6.4 %fusion.13 = f32[6,3,32768]{2,0,1:T(8,128)S(1)} fusion(f32[8,3,32768]{2,1,0:T(4,128)} %all_to_all.10, f32[6,8]{1,0:T(8,128)S(1)} %fusion.51), kind=kOutput, calls=%fused_computation.14 | convolution fusion | flops 56623104 | bytes 5505216 | tf_op jit(solution)/shard_map/sq,src->qrc/dot_general | solution.py:41
  582.9 3.3 copy.56
  586.2 0.7 copy.57
  (48 shorter events, 3.3 us)
Async XLA Ops:
  7.2 0.7 copy-start
  7.2 132.8 %all-gather.10.cloned.1.call-start = ((), (), s32[]{:S(2)}) async-start(), calls=%async_computation.1 | async-start | bytes 3158016 | tf_op jit(solution)/shard_map/all_gather | solution.py:12
  13.7 7.9 %copy-start.1 = (f32[1,80,32768]{2,1,0:T(8,128)S(1)}, f32[1,80,32768]{2,1,0:T(8,128)}, u32[]{:S(2)}) copy-start(f32[1,80,32768]{2,1,0:T(8,128)} %param.9) | copy-start | bytes 31457284
  30.5 241.1 %all-gather.12.cloned.1.call-start = ((), (), s32[]{:S(2)}) async-start(), calls=%async_computation.2 | async-start | bytes 3158016 | tf_op jit(solution)/shard_map/all_gather | solution.py:12
  167.3 236.0 %all-gather.14.cloned.1.call-start = ((), (), s32[]{:S(2)}) async-start(), calls=%async_computation.3 | async-start | bytes 3158016 | tf_op jit(solution)/shard_map/all_gather | solution.py:12
  411.3 7.8 %copy-start.2 = (f32[80,24]{0,1:T(8,128)}, f32[80,24]{0,1:T(8,128)S(1)}, u32[]{:S(2)}) copy-start(f32[80,24]{0,1:T(8,128)S(1)} %convolution_bitcast_fusion.1) | copy-start | bytes 23044
  424.0 5.2 copy-start.3
  424.0 42.3 %all-to-all-start = ((f32[1,24,32768]{2,0,1:T(1,128)}), f32[1,24,32768]{2,0,1:T(1,128)}, u32[]{:S(2)}, u32[]{:S(2)}) async-start(f32[1,24,32768]{2,0,1:T(1,128)} %copy.44), calls=%async_computation | async-start | bytes 6291456 | tf_op jit(solution)/shard_map/all_to_all | solution.py:35
Sparse Core Ops, SparseCore 0:
  30.6 109.3 all-gather.9
  167.4 104.1 all-gather.11
  299.1 104.1 all-gather.13
